TPU v7x, 32 devices: a whole 2x2x4 slice. The times are simulated.
32 devices in a mesh: dp: 8 (over z, y), mp: 4 (over x, core).
Axes of the slice: x: 2, y: 2, z: 4, core: 2. Of those that a mesh axis runs over, the one named last changes fastest.
Arguments:
- token_ids: int32 [16384], P('dp'), may hold values from 0 to 8191
- seg_ids: int32 [16384], P('dp'), may hold values from 0 to 255, as said below
- timesteps: int32 [16384], P('dp'), may hold values from 0 to 1999
- noise: float32 [16384, 128], P('dp'), may hold values from -6 to 6
- table: bfloat16 [8192, 128], P('dp'), may hold values from -6 to 6
- w_in: bfloat16 [128, 768], replicated, may hold values from -0.5 to 0.5
- b_in: float32 [768], replicated, may hold values from -3 to 3
- w_time: bfloat16 [128, 768], replicated, may hold values from -0.5 to 0.5
- gain1: float32 [768], replicated, may hold values from 0.5 to 1.5
- shift1: float32 [768], replicated, may hold values from -2 to 2
- w_qkv: bfloat16 [3, 768, 768], P(None, None, 'mp'), may hold values from -0.21875 to 0.21875
- w_out: bfloat16 [768, 768], P('mp'), may hold values from -3.5 to 3.5
- gain2: float32 [768], replicated, may hold values from 0.5 to 1.5
- shift2: float32 [768], replicated, may hold values from -2 to 2
- w_up: bfloat16 [768, 3072], P(None, 'mp'), may hold values from -0.21875 to 0.21875
- b_up: float32 [3072], P('mp'), may hold values from -2 to 2
- w_down: bfloat16 [3072, 768], P('mp'), may hold values from -0.109375 to 0.109375
- b_down: float32 [768], replicated, may hold values from -2 to 2
- cotangent: float32 [16384, 768], P('dp'), may hold values from -6 to 6
Outputs:
- output: float32 [16384, 768], P('dp')
- grad_table: float32 [8192, 128], P('dp')
- grad_w_in: float32 [128, 768], replicated
- grad_b_in: float32 [768], replicated
- grad_w_time: float32 [128, 768], replicated
- grad_gain1: float32 [768], replicated
- grad_shift1: float32 [768], replicated
- grad_w_qkv: float32 [3, 768, 768], P(None, None, 'mp')
- grad_w_out: float32 [768, 768], P('mp')
- grad_gain2: float32 [768], replicated
- grad_shift2: float32 [768], replicated
- grad_w_up: float32 [768, 3072], P(None, 'mp')
- grad_b_up: float32 [3072], P('mp')
- grad_w_down: float32 [3072, 768], P('mp')
- grad_b_down: float32 [768], replicated
Inputs may be any that keep to these rules, and one draw needn't show every extreme that they name: `seg_ids`: slots fall into aligned runs of 1024; each run is either one document or 16 documents of 64 slots; ids never fall along the slots and differ between runs; the first run is one document and the last is split.
All inputs are finite; a program needn't handle non-finite values.
Results may differ from a plain program's by a relative error of at most 0.017.
Values may be sent and summed in bfloat16 or wider, within the bound.
No kernel may reach another device: no remote copies, remote signals or barrier semaphores. Data moves between devices by JAX's collectives and lax.ppermute only.
A program may use at most 192 MiB of HBM per device.

v0:
```python
import math
import jax
import jax.numpy as jnp
from jax import lax
from jax.sharding import PartitionSpec as P

HD = 64
TSTEPS = 2000
QBLK = 512
NEG_BIG = -1000000000.0


def layer_norm(inputs, gain_vec, shift_vec):
    row_mean = jnp.mean(inputs, axis=-1, keepdims=True)
    centred = inputs - row_mean
    variance = jnp.mean(centred * centred, axis=-1, keepdims=True)
    return centred * lax.rsqrt(variance + 1e-05) * gain_vec + shift_vec


def noise_rates(time_ids, horizon):
    fraction = time_ids.astype(jnp.float32) / horizon
    signal = 1.0 - jnp.sqrt(fraction + 0.0001)
    return (jnp.sqrt(signal), jnp.sqrt(1.0 - signal))


def time_features(time_ids, feat_width):
    half_width = feat_width // 2
    freq_table = jnp.exp(
        -math.log(10000.0) * jnp.arange(half_width, dtype=jnp.float32) / half_width
    )
    angles = time_ids.astype(jnp.float32)[:, None] * freq_table[None, :]
    return jnp.concatenate([jnp.sin(angles), jnp.cos(angles)], axis=1)


def gelu_exact(inputs):
    return jax.nn.gelu(inputs, approximate=False)


def block_rows(array_in, index, block_len):
    return lax.dynamic_slice_in_dim(array_in, index * block_len, block_len, 0)


def masked_scores(query_blk, key_blk, seg_query, seg_key):
    scaled = jnp.einsum(
        "qhd,khd->hqk", query_blk, key_blk, preferred_element_type=jnp.float32
    ) * query_blk.shape[-1] ** (-0.5)
    same_seg = seg_query[:, None] == seg_key[None, :]
    return jnp.where(same_seg[None], scaled, NEG_BIG)


def attend_forward(queries, keys_all, values_all, seg_ids, block_len):
    token_count, head_count, head_width = queries.shape
    block_count = token_count // block_len

    def query_block(q_index):
        query_blk = block_rows(queries, q_index, block_len)
        seg_query = block_rows(seg_ids, q_index, block_len)

        def stats_step(k_index, current):
            row_top, row_sum = current
            scores = masked_scores(
                query_blk,
                block_rows(keys_all, k_index, block_len),
                seg_query,
                block_rows(seg_ids, k_index, block_len),
            )
            new_top = jnp.maximum(row_top, jnp.max(scores, axis=-1))
            new_sum = row_sum * jnp.exp(row_top - new_top) + jnp.sum(
                jnp.exp(scores - new_top[:, :, None]), axis=-1
            )
            return (new_top, new_sum)

        start_stats = (
            jnp.full((head_count, block_len), NEG_BIG, jnp.float32),
            jnp.zeros((head_count, block_len), jnp.float32),
        )
        row_top, row_sum = lax.fori_loop(0, block_count, stats_step, start_stats)

        def value_step(k_index, current):
            scores = masked_scores(
                query_blk,
                block_rows(keys_all, k_index, block_len),
                seg_query,
                block_rows(seg_ids, k_index, block_len),
            )
            weights_bf = (jnp.exp(scores - row_top[:, :, None]) / row_sum[:, :, None]).astype(
                jnp.bfloat16
            )
            return current + jnp.einsum(
                "hqk,khd->qhd",
                weights_bf,
                block_rows(values_all, k_index, block_len),
                preferred_element_type=jnp.float32,
            )

        mixed_blk = lax.fori_loop(
            0, block_count, value_step, jnp.zeros((block_len, head_count, head_width), jnp.float32)
        )
        return (mixed_blk, row_top, row_sum)

    mixed_all, tops, sums = lax.map(query_block, jnp.arange(block_count))
    return (mixed_all.reshape(token_count, head_count, head_width), tops, sums)


def attend_backward(queries, keys_all, values_all, grad_mixed, seg_ids, tops, sums, block_len):
    token_count, head_count, head_width = queries.shape
    block_count = token_count // block_len
    scale_factor = head_width ** (-0.5)

    def query_step(q_index, totals):
        grad_q_all, grad_k_all, grad_v_all = totals
        query_blk = block_rows(queries, q_index, block_len)
        grad_blk = block_rows(grad_mixed, q_index, block_len)
        seg_query = block_rows(seg_ids, q_index, block_len)
        row_top = tops[q_index]
        row_sum = sums[q_index]

        def probs_for(k_index):
            key_blk = block_rows(keys_all, k_index, block_len)
            value_blk = block_rows(values_all, k_index, block_len)
            scores = masked_scores(
                query_blk, key_blk, seg_query, block_rows(seg_ids, k_index, block_len)
            )
            weights = jnp.exp(scores - row_top[:, :, None]) / row_sum[:, :, None]
            grad_weights = jnp.einsum(
                "qhd,khd->hqk", grad_blk, value_blk, preferred_element_type=jnp.float32
            )
            return (key_blk, weights, grad_weights)

        def delta_step(k_index, current):
            key_blk, weights, grad_weights = probs_for(k_index)
            return current + jnp.sum(grad_weights * weights, axis=-1)

        delta = lax.fori_loop(
            0, block_count, delta_step, jnp.zeros((head_count, block_len), jnp.float32)
        )

        def grad_step(k_index, current):
            grad_query, grad_keys, grad_values = current
            key_blk, weights, grad_weights = probs_for(k_index)
            grad_scores = (weights * (grad_weights - delta[:, :, None])).astype(jnp.bfloat16)
            grad_query = (
                grad_query
                + jnp.einsum(
                    "hqk,khd->qhd", grad_scores, key_blk, preferred_element_type=jnp.float32
                )
                * scale_factor
            )
            key_part = (
                jnp.einsum(
                    "hqk,qhd->khd", grad_scores, query_blk, preferred_element_type=jnp.float32
                )
                * scale_factor
            )
            value_part = jnp.einsum(
                "hqk,qhd->khd",
                weights.astype(jnp.bfloat16),
                grad_blk,
                preferred_element_type=jnp.float32,
            )
            grad_keys = lax.dynamic_update_slice_in_dim(
                grad_keys,
                block_rows(grad_keys, k_index, block_len) + key_part,
                k_index * block_len,
                0,
            )
            grad_values = lax.dynamic_update_slice_in_dim(
                grad_values,
                block_rows(grad_values, k_index, block_len) + value_part,
                k_index * block_len,
                0,
            )
            return (grad_query, grad_keys, grad_values)

        start_grads = (
            jnp.zeros((block_len, head_count, head_width), jnp.float32),
            grad_k_all,
            grad_v_all,
        )
        grad_query, grad_k_all, grad_v_all = lax.fori_loop(0, block_count, grad_step, start_grads)
        grad_q_all = lax.dynamic_update_slice_in_dim(grad_q_all, grad_query, q_index * block_len, 0)
        return (grad_q_all, grad_k_all, grad_v_all)

    zeros_all = jnp.zeros(queries.shape, jnp.float32)
    return lax.fori_loop(0, block_count, query_step, (zeros_all, zeros_all, zeros_all))


def body(
    token_ids,
    seg_ids,
    timesteps,
    noise,
    table,
    w_in,
    b_in,
    w_time,
    gain1,
    shift1,
    w_qkv,
    w_out,
    gain2,
    shift2,
    w_up,
    b_up,
    w_down,
    b_down,
    cotangent,
):
    whole_table = lax.all_gather(table, "dp", axis=0, tiled=True)
    table_full = whole_table.astype(jnp.float32)
    vocab_rows, embed_width = table_full.shape
    row_norms = jnp.sqrt(jnp.sum(table_full * table_full, axis=1) + 1e-06)
    mean_norm = jnp.mean(row_norms)
    factor = math.sqrt(embed_width) / mean_norm
    looked_up = jnp.take(table_full, token_ids, axis=0)
    clean_rows = looked_up * factor
    keep_rate, noise_rate = noise_rates(timesteps, TSTEPS)
    noisy_in = (keep_rate[:, None] * clean_rows + noise_rate[:, None] * noise).astype(jnp.bfloat16)
    features = time_features(timesteps, w_time.shape[0]).astype(jnp.bfloat16)
    hidden = (
        jnp.dot(noisy_in, w_in, preferred_element_type=jnp.float32)
        + jnp.dot(features, w_time, preferred_element_type=jnp.float32)
        + b_in
    )
    token_count = hidden.shape[0]
    act_one_f, norm_one_back = jax.vjp(layer_norm, hidden, gain1, shift1)
    act_one = act_one_f.astype(jnp.bfloat16)
    projected = jnp.einsum(
        "td,cdk->ctk", act_one, w_qkv, preferred_element_type=jnp.float32
    ).astype(jnp.bfloat16)
    head_count = w_qkv.shape[2] // HD
    heads_all = projected.reshape(3, token_count, head_count, HD)
    queries, keys_all, values_all = (heads_all[0], heads_all[1], heads_all[2])
    mixed_f, tops, sums = attend_forward(queries, keys_all, values_all, seg_ids, QBLK)
    mixed = mixed_f.astype(jnp.bfloat16).reshape(token_count, head_count * HD)
    attn_part = jnp.dot(mixed, w_out, preferred_element_type=jnp.float32)
    resid = hidden + lax.psum(attn_part, "mp")
    act_two_f, norm_two_back = jax.vjp(layer_norm, resid, gain2, shift2)
    act_two = act_two_f.astype(jnp.bfloat16)
    pre_act = jnp.dot(act_two, w_up, preferred_element_type=jnp.float32) + b_up
    activated_f, gelu_back = jax.vjp(gelu_exact, pre_act)
    activated = activated_f.astype(jnp.bfloat16)
    down_part = jnp.dot(activated, w_down, preferred_element_type=jnp.float32)
    output = resid + lax.psum(down_part.astype(jnp.bfloat16), "mp").astype(jnp.float32) + b_down
    cot_rounded = cotangent.astype(jnp.bfloat16)
    grad_w_down = jnp.einsum(
        "tf,td->fd", activated, cot_rounded, preferred_element_type=jnp.float32
    )
    grad_b_down = jnp.sum(cotangent, axis=0)
    grad_gelu = jnp.einsum("td,fd->tf", cot_rounded, w_down, preferred_element_type=jnp.float32)
    (grad_pre,) = gelu_back(grad_gelu)
    grad_pre_r = grad_pre.astype(jnp.bfloat16)
    grad_w_up = jnp.einsum("td,tf->df", act_two, grad_pre_r, preferred_element_type=jnp.float32)
    grad_b_up = jnp.sum(grad_pre_r.astype(jnp.float32), axis=0)
    grad_two_part = jnp.einsum("tf,df->td", grad_pre_r, w_up, preferred_element_type=jnp.float32)
    grad_act_two = lax.psum(grad_two_part, "mp")
    grad_resid_norm, grad_gain2, grad_shift2 = norm_two_back(grad_act_two)
    grad_resid = cotangent + grad_resid_norm
    grad_attn_r = grad_resid.astype(jnp.bfloat16)
    grad_w_out = jnp.einsum("tk,td->kd", mixed, grad_attn_r, preferred_element_type=jnp.float32)
    grad_mixed = (
        jnp.einsum("td,kd->tk", grad_attn_r, w_out, preferred_element_type=jnp.float32)
        .astype(jnp.bfloat16)
        .reshape(token_count, head_count, HD)
    )
    grad_q, grad_k, grad_v = attend_backward(
        queries, keys_all, values_all, grad_mixed, seg_ids, tops, sums, QBLK
    )
    grad_proj = jnp.stack(
        [grad_q.astype(jnp.bfloat16), grad_k.astype(jnp.bfloat16), grad_v.astype(jnp.bfloat16)]
    ).reshape(3, token_count, head_count * HD)
    grad_w_qkv = jnp.einsum("td,ctk->cdk", act_one, grad_proj, preferred_element_type=jnp.float32)
    grad_one_part = jnp.einsum("ctk,cdk->td", grad_proj, w_qkv, preferred_element_type=jnp.float32)
    grad_act_one = lax.psum(grad_one_part.astype(jnp.bfloat16), "mp").astype(jnp.float32)
    grad_hidden_norm, grad_gain1, grad_shift1 = norm_one_back(grad_act_one)
    grad_hidden_r = (grad_resid + grad_hidden_norm).astype(jnp.bfloat16)
    grad_w_in = jnp.einsum("te,td->ed", noisy_in, grad_hidden_r, preferred_element_type=jnp.float32)
    grad_w_time = jnp.einsum(
        "te,td->ed", features, grad_hidden_r, preferred_element_type=jnp.float32
    )
    grad_b_in = jnp.sum(grad_hidden_r.astype(jnp.float32), axis=0)
    grad_noisy = jnp.einsum("td,ed->te", grad_hidden_r, w_in, preferred_element_type=jnp.float32)
    grad_clean = keep_rate[:, None] * grad_noisy
    scaled_grad = grad_clean * factor
    norm_coeff = -jnp.sum(grad_clean * looked_up) * factor / (mean_norm * vocab_rows)
    unit_rows = table_full / row_norms[:, None]
    row_count = lax.axis_size("dp") * table.shape[0]
    inside = (token_ids >= 0) & (token_ids < row_count)
    slot_ids = jnp.where(inside, token_ids, row_count)
    direct = jax.ops.segment_sum(scaled_grad, slot_ids, num_segments=row_count + 1)[:row_count]
    grad_table = lax.psum_scatter(
        direct + norm_coeff * unit_rows, "dp", scatter_dimension=0, tiled=True
    )
    summed = tuple(
        lax.psum(
            (
                grad_w_in,
                grad_b_in,
                grad_w_time,
                grad_gain1,
                grad_shift1,
                grad_w_qkv,
                grad_w_out,
                grad_gain2,
                grad_shift2,
                grad_w_up,
                grad_b_up,
                grad_w_down,
                grad_b_down,
            ),
            "dp",
        )
    )
    return (
        output,
        grad_table,
        summed[0],
        summed[1],
        summed[2],
        summed[3],
        summed[4],
        summed[5],
        summed[6],
        summed[7],
        summed[8],
        summed[9],
        summed[10],
        summed[11],
        summed[12],
    )


def solution(mesh):
    in_specs = (
        P("dp"),
        P("dp"),
        P("dp"),
        P("dp", None),
        P("dp", None),
        P(),
        P(),
        P(),
        P(),
        P(),
        P(None, None, "mp"),
        P("mp", None),
        P(),
        P(),
        P(None, "mp"),
        P("mp"),
        P("mp", None),
        P(),
        P("dp", None),
    )
    out_specs = (
        P("dp", None),
        P("dp", None),
        P(),
        P(),
        P(),
        P(),
        P(),
        P(None, None, "mp"),
        P("mp", None),
        P(),
        P(),
        P(None, "mp"),
        P("mp"),
        P("mp", None),
        P(),
    )
    return jax.shard_map(body, mesh=mesh, in_specs=in_specs, out_specs=out_specs, check_vma=False)
```

profile of v0, /device:TPU:0, one launch (start us, length us, event | category | flops | bytes accessed | tf_op | source)
XLA Modules:
  0.0 1170.5 jit_solution(15731865098663500380)
XLA Ops:
  13.5 48.5 %all-gather.2.cloned.1.call-done = bf16[8192,128]{1,0:T(8,128)(2,1)} async-done(((bf16[1024,128]{1,0:T(8,128)(2,1)}), bf16[8192,128]{1,0:T(8,128)(2,1)}) %all-gather.2.cloned.1.call-update) | async-done | bytes 2097168 | tf_op jit(solution)/shard_map/all_gather | solution.py:209
  90.6 98.2 %while.123 = (s32[]{:T(128)}, bf16[4,512,3,64]{1,3,2,0:T(8,128)(2,1)}, f32[4,3,512]{2,1,0:T(4,128)}, f32[4,3,512]{2,1,0:T(4,128)}, s32[4]{0:T(128)S(1)}, /*index...) while((s32[]{:T(128)}, ...), condition=%wide.region_11.12_spmd, body=%wide.region_4.11_spmd.sunk | while | flops 312155648 | bytes 10699101 | solution.py:101
  100.9 12.5 %while.128 = (s32[]{:T(128)}, f32[512,3,64]{0,2,1:T(8,128)}, bf16[2048,3,64]{0,2,1:T(8,128)(2,1)S(1)}, s32[512]{0:T(512)S(1)}, s32[2048]{0:T(1024)S(1)}, /*index...) while((s32[]{:T(128)}, f32[512,3,64]{0,2,1:T(8,128)}, ...), condition=%wide.region_10.10_spmd.clone, body=%wide.region_9.9_spmd.clone.sunk | while | flops 205717504 | bytes 1926848 | solution.py:96
  125.4 12.5 %while.128 = (s32[]{:T(128)}, f32[512,3,64]{0,2,1:T(8,128)}, bf16[2048,3,64]{0,2,1:T(8,128)(2,1)S(1)}, s32[512]{0:T(512)S(1)}, s32[2048]{0:T(1024)S(1)}, /*index...) while((s32[]{:T(128)}, f32[512,3,64]{0,2,1:T(8,128)}, ...), condition=%wide.region_10.10_spmd.clone, body=%wide.region_9.9_spmd.clone.sunk | while | flops 205717504 | bytes 1926848 | solution.py:96
  149.8 12.5 %while.128 = (s32[]{:T(128)}, f32[512,3,64]{0,2,1:T(8,128)}, bf16[2048,3,64]{0,2,1:T(8,128)(2,1)S(1)}, s32[512]{0:T(512)S(1)}, s32[2048]{0:T(1024)S(1)}, /*index...) while((s32[]{:T(128)}, f32[512,3,64]{0,2,1:T(8,128)}, ...), condition=%wide.region_10.10_spmd.clone, body=%wide.region_9.9_spmd.clone.sunk | while | flops 205717504 | bytes 1926848 | solution.py:96
  174.3 12.5 %while.128 = (s32[]{:T(128)}, f32[512,3,64]{0,2,1:T(8,128)}, bf16[2048,3,64]{0,2,1:T(8,128)(2,1)S(1)}, s32[512]{0:T(512)S(1)}, s32[2048]{0:T(1024)S(1)}, /*index...) while((s32[]{:T(128)}, f32[512,3,64]{0,2,1:T(8,128)}, ...), condition=%wide.region_10.10_spmd.clone, body=%wide.region_9.9_spmd.clone.sunk | while | flops 205717504 | bytes 1926848 | solution.py:96
  195.6 118.2 %all-reduce.8.cloned.1.call-done = f32[2048,768]{0,1:T(8,128)} async-done(((f32[2048,768]{0,1:T(8,128)}), f32[2048,768]{0,1:T(8,128)}) %all-reduce.8.cloned.1.call-update) | async-done | bytes 6291472 | tf_op jit(solution)/shard_map/psum | solution.py:237
  323.0 18.8 %multiply_convert_fusion = (bf16[2048,768]{1,0:T(8,128)(2,1)}, f32[2048,768]{1,0:T(8,128)}, f32[2048,768]{1,0:T(8,128)}) fusion(f32[768]{0:T(1024)S(1)} %copy-done.63, bf16[2048,768]{0,1:T(8,128)(2,1)S(1)} %add_convert_fusion.2, bf16[768,768]{1,0:T(8,128)(2,1)S(1)} %copy-done), kind=kOutput, calls=%fused_computation.93 | convolution fusion | flops 2519728128 | bytes 20057088 | tf_op jit(solution)/shard_map/dot_general | solution.py:240
  341.8 8.1 convert_reduce_fusion.1
  370.1 105.9 %all-reduce.10.cloned.1.call-done = f32[2048,768]{0,1:T(8,128)} async-done(((f32[2048,768]{0,1:T(8,128)}), f32[2048,768]{0,1:T(8,128)}) %all-reduce.10.cloned.1.call-update) | async-done | bytes 6291472 | tf_op jit(solution)/shard_map/psum | solution.py:256
  492.9 161.6 %while.126 = (s32[]{:T(128)}, bf16[2048,3,64]{0,2,1:T(8,128)(2,1)}, f32[2048,3,64]{0,2,1:T(8,128)}, f32[2048,3,64]{0,2,1:T(8,128)S(1)}, bf16[2048,3,64]{0,2,1:T(...) while((s32[]{:T(128)}, bf16[2048,3,64]{0,2,1:T(8,128)(2,1)}, ...), condition=%wide.region_25.26_spmd, body=%wide.region_19.25_spmd.sunk | while | flops 716768768 | bytes 27696096 | solution.py:185
  494.7 12.6 %while.129 = (s32[]{:T(128)}, f32[3,512]{1,0:T(4,128)S(1)}, bf16[2048,3,64]{0,2,1:T(8,128)(2,1)}, bf16[512,3,64]{0,2,1:T(8,128)(2,1)S(1)}, s32[512]{0:T(512)S(1)...) while((s32[]{:T(128)}, f32[3,512]{1,0:T(4,128)S(1)}, ...), condition=%wide.region_22.22_spmd.clone, body=%wide.region_20.21_spmd.clone.sunk | while | flops 206308864 | bytes 7647441 | solution.py:134
  507.3 25.2 %while.130 = (s32[]{:T(128)}, f32[512,3,64]{0,2,1:T(8,128)S(1)}, f32[2048,3,64]{0,2,1:T(8,128)}, f32[2048,3,64]{0,2,1:T(8,128)S(1)}, bf16[2048,3,64]{0,2,1:T(8,1...) while((s32[]{:T(128)}, f32[512,3,64]{0,2,1:T(8,128)S(1)}, ...), condition=%wide.region_24.24_spmd.clone, body=%wide.region_23.23_spmd.clone.sunk | while | flops 510459904 | bytes 18446580 | solution.py:180
  535.1 12.6 %while.129 = (s32[]{:T(128)}, f32[3,512]{1,0:T(4,128)S(1)}, bf16[2048,3,64]{0,2,1:T(8,128)(2,1)}, bf16[512,3,64]{0,2,1:T(8,128)(2,1)S(1)}, s32[512]{0:T(512)S(1)...) while((s32[]{:T(128)}, f32[3,512]{1,0:T(4,128)S(1)}, ...), condition=%wide.region_22.22_spmd.clone, body=%wide.region_20.21_spmd.clone.sunk | while | flops 206308864 | bytes 7647441 | solution.py:134
  547.7 25.2 %while.130 = (s32[]{:T(128)}, f32[512,3,64]{0,2,1:T(8,128)S(1)}, f32[2048,3,64]{0,2,1:T(8,128)}, f32[2048,3,64]{0,2,1:T(8,128)S(1)}, bf16[2048,3,64]{0,2,1:T(8,1...) while((s32[]{:T(128)}, f32[512,3,64]{0,2,1:T(8,128)S(1)}, ...), condition=%wide.region_24.24_spmd.clone, body=%wide.region_23.23_spmd.clone.sunk | while | flops 510459904 | bytes 18446580 | solution.py:180
  575.5 12.6 %while.129 = (s32[]{:T(128)}, f32[3,512]{1,0:T(4,128)S(1)}, bf16[2048,3,64]{0,2,1:T(8,128)(2,1)}, bf16[512,3,64]{0,2,1:T(8,128)(2,1)S(1)}, s32[512]{0:T(512)S(1)...) while((s32[]{:T(128)}, f32[3,512]{1,0:T(4,128)S(1)}, ...), condition=%wide.region_22.22_spmd.clone, body=%wide.region_20.21_spmd.clone.sunk | while | flops 206308864 | bytes 7647441 | solution.py:134
  588.1 25.2 %while.130 = (s32[]{:T(128)}, f32[512,3,64]{0,2,1:T(8,128)S(1)}, f32[2048,3,64]{0,2,1:T(8,128)}, f32[2048,3,64]{0,2,1:T(8,128)S(1)}, bf16[2048,3,64]{0,2,1:T(8,1...) while((s32[]{:T(128)}, f32[512,3,64]{0,2,1:T(8,128)S(1)}, ...), condition=%wide.region_24.24_spmd.clone, body=%wide.region_23.23_spmd.clone.sunk | while | flops 510459904 | bytes 18446580 | solution.py:180
  615.9 12.6 %while.129 = (s32[]{:T(128)}, f32[3,512]{1,0:T(4,128)S(1)}, bf16[2048,3,64]{0,2,1:T(8,128)(2,1)}, bf16[512,3,64]{0,2,1:T(8,128)(2,1)S(1)}, s32[512]{0:T(512)S(1)...) while((s32[]{:T(128)}, f32[3,512]{1,0:T(4,128)S(1)}, ...), condition=%wide.region_22.22_spmd.clone, body=%wide.region_20.21_spmd.clone.sunk | while | flops 206308864 | bytes 7647441 | solution.py:134
  628.4 25.2 %while.130 = (s32[]{:T(128)}, f32[512,3,64]{0,2,1:T(8,128)S(1)}, f32[2048,3,64]{0,2,1:T(8,128)}, f32[2048,3,64]{0,2,1:T(8,128)S(1)}, bf16[2048,3,64]{0,2,1:T(8,1...) while((s32[]{:T(128)}, f32[512,3,64]{0,2,1:T(8,128)S(1)}, ...), condition=%wide.region_24.24_spmd.clone, body=%wide.region_23.23_spmd.clone.sunk | while | flops 510459904 | bytes 18446580 | solution.py:180
  682.7 100.5 %all-reduce.14.cloned.1.call-done = (bf16[2048,768]{0,1:T(8,128)(2,1)}, bf16[2048,768]{0,1:T(8,128)(2,1)}) async-done(((bf16[2048,768]{0,1:T(8,128)(2,1)}, bf16[2048,768]{0,1:T(8,128)(2,1)}), (bf16[2048,768]{0,1:T(8,128)(2,1)}, bf16[2048,768]{0,1:T(8,128)(2,1)})) %all-reduce.14.cloned.1.call-update) | async-done | bytes 6291472 | tf_op jit(solution)/shard_map/psum | solution.py:244
  811.0 13.1 %scatter_custom_fusion = f32[8193,128]{1,0:T(8,128)} fusion(s32[2048]{0:T(1024)} %get-tuple-element.1347, f32[]{:T(128)} %constant.325.clone.1, f32[2048,128]{1,0:T(8,128)} %get-tuple-element.1355, f32[]{:T(128)S(6)} %div.136), kind=kCustom, calls=%fused_computation.122 | custom fusion | flops 524288 | bytes 5243908 | tf_op jit(solution)/shard_map/scatter-add | solution.py:290
  847.8 40.1 %all-reduce = (f32[768]{0:T(1024)}, f32[768]{0:T(1024)}, f32[768]{0:T(1024)}, f32[768]{0:T(1024)}, f32[768]{0:T(1024)}, /*index=5*/f32[768]{0:T(1024)}, f32[768]{0:T(1024)}) all-reduce(f32[768]{0:T(1024)S(1)} %get-tuple-element.1324, f32[768]{0:T(1024)S(1)} %get-tuple-element.1186, ...), channel_id=1, replica_groups=mesh['dp'=8,'mp'=4] {'dp'}, use_global_device_ids=true, to_apply=%region_34.35 | all-reduce | flops 5376 | bytes 43008 | tf_op jit(solution)/shard_map/psum | solution.py:295
  887.9 172.8 %all-reduce.12.cloned.1.call-done = (f32[128,768]{1,0:T(8,128)}, f32[128,768]{1,0:T(8,128)}, f32[3,768,192]{1,2,0:T(8,128)}, f32[192,768]{1,0:T(8,128)}, f32[768,768]{1,0:T(8,128)}, /*index=5*/f32[768,768]{1,0:T(8,128)}) async-done(((f32[128,768]{1,0:T(8,128)}, f32[128,768]{1,0:T(8,128)}, f32[3,768,192]{1,2,0:T(8,128)}, f32[192,768]{1,0:T(8,128)}, f32[768,768]{1,0:T(8,128)}, ...) | async-done | bytes 7864336 | tf_op jit(solution)/shard_map/psum | solution.py:295
  1060.6 91.4 %reduce-scatter.2.cloned.1.call-done = f32[1024,128]{1,0:T(8,128)} async-done(((f32[8192,128]{1,0:T(8,128)}), f32[1024,128]{1,0:T(8,128)}) %reduce-scatter.2.cloned.1.call-update) | async-done | bytes 524304 | tf_op jit(solution)/shard_map/reduce_scatter | solution.py:291
  (643 shorter events, 459.9 us)
Async XLA Ops:
  7.2 315.8 %copy-start = (bf16[768,768]{1,0:T(8,128)(2,1)S(1)}, bf16[768,768]{1,0:T(8,128)(2,1)}, u32[]{:S(2)}) copy-start(bf16[768,768]{1,0:T(8,128)(2,1)} %param.45) | copy-start | bytes 3538948
  7.2 54.8 %all-gather.2.cloned.1.call-start = ((), (), s32[]{:S(2)}) async-start(), calls=%async_computation.1 | async-start | bytes 2359296 | tf_op jit(solution)/shard_map/all_gather | solution.py:209
  7.9 305.9 %all-reduce.8.cloned.1.call-start = ((), (), s32[]{:S(2)}) async-start(), calls=%async_computation.2 | async-start | bytes 12582912 | tf_op jit(solution)/shard_map/psum | solution.py:237
  9.4 68.8 %copy-start.51 = (pred[2048]{0:T(1024)(128)(4,1)}, pred[2048]{0:T(1024)(128)(4,1)S(1)}, u32[]{:S(2)}) copy-start(pred[2048]{0:T(1024)(128)(4,1)S(1)} %compare_and_fusion) | copy-start | bytes 6148
  11.4 66.8 %copy-start.39 = (f32[2048]{0:T(1024)}, f32[2048]{0:T(1024)S(1)}, u32[]{:S(2)}) copy-start(f32[2048]{0:T(1024)S(1)} %get-tuple-element.1349) | copy-start | bytes 24580
  13.5 69.2 %copy-start.23 = (bf16[2048,64]{0,1:T(8,128)(2,1)}, bf16[2048,64]{0,1:T(8,128)(2,1)S(1)}, u32[]{:S(2)}) copy-start(bf16[2048,64]{0,1:T(8,128)(2,1)S(1)} %get-tuple-element.1345) | copy-start | bytes 786436
  13.5 69.2 %copy-start.25 = (bf16[2048,64]{0,1:T(8,128)(2,1)}, bf16[2048,64]{0,1:T(8,128)(2,1)S(1)}, u32[]{:S(2)}) copy-start(bf16[2048,64]{0,1:T(8,128)(2,1)S(1)} %get-tuple-element.1346) | copy-start | bytes 786436
  90.5 101.3 %copy-start.29 = (bf16[192,768]{1,0:T(8,128)(2,1)S(1)}, bf16[192,768]{1,0:T(8,128)(2,1)}, u32[]{:S(2)}) copy-start(bf16[192,768]{1,0:T(8,128)(2,1)} %param.42) | copy-start | bytes 884740
  195.6 280.5 %all-reduce.10.cloned.1.call-start = ((), (), s32[]{:S(2)}) async-start(), calls=%async_computation.3 | async-start | bytes 12582912 | tf_op jit(solution)/shard_map/psum | solution.py:256
  320.8 20.9 %slice-start.2 = ((s8[6291456]{0:T(1024)(128)(4,1)}), s8[4194304]{0:T(1024)(128)(4,1)S(1)}, s32[]{:S(2)}) async-start(s8[6291456]{0:T(1024)(128)(4,1)} %bitcast.204), calls=%async_computation.9 | async-start | bytes 8388608
  322.9 18.8 %copy-start.21 = (bf16[2048,768]{0,1:T(8,128)(2,1)}, bf16[2048,768]{0,1:T(8,128)(2,1)S(1)}, u32[]{:S(2)}) copy-start(bf16[2048,768]{0,1:T(8,128)(2,1)S(1)} %add_convert_fusion.2) | copy-start | bytes 9437188
  322.9 18.8 %slice-start.3 = ((s8[6291456]{0:T(1024)(128)(4,1)}), s8[2097152]{0:T(1024)(128)(4,1)S(1)}, s32[]{:S(2)}) async-start(s8[6291456]{0:T(1024)(128)(4,1)} %bitcast.204), calls=%async_computation.10 | async-start | bytes 4194304
  322.9 18.8 %copy-start.61 = (bf16[768,768]{1,0:T(8,128)(2,1)S(1)}, bf16[768,768]{1,0:T(8,128)(2,1)}, u32[]{:S(2)}) copy-start(bf16[768,768]{1,0:T(8,128)(2,1)} %param.47) | copy-start | bytes 3538948
  356.1 427.0 %all-reduce.14.cloned.1.call-start = ((), (), s32[]{:S(2)}) async-start(), calls=%async_computation.6 | async-start | bytes 12582912 | tf_op jit(solution)/shard_map/psum | solution.py:244
  663.2 397.5 %all-reduce.12.cloned.1.call-start = ((), (), s32[]{:S(2)}) async-start(), calls=%async_computation.5 | async-start | bytes 15728640 | tf_op jit(solution)/shard_map/psum | solution.py:295
  679.4 103.8 %copy-start.38 = (f32[2048]{0:T(1024)S(1)}, f32[2048]{0:T(1024)}, u32[]{:S(2)}) copy-start(f32[2048]{0:T(1024)} %copy-done.37) | copy-start | bytes 24580
  679.4 103.7 %copy-start.50 = (f32[768]{0:T(1024)S(1)}, f32[768]{0:T(1024)}, u32[]{:S(2)}) copy-start(f32[768]{0:T(1024)} %param.39) | copy-start | bytes 9220
  679.4 115.2 %slice-start.6 = ((s8[6291456]{0:T(1024)(128)(4,1)}), s8[2097152]{0:T(1024)(128)(4,1)S(1)}, s32[]{:S(2)}) async-start(s8[6291456]{0:T(1024)(128)(4,1)} %bitcast.208), calls=%async_computation.13 | async-start | bytes 4194304
  682.7 106.2 %copy-start.48 = (f32[2048]{0:T(1024)S(1)}, f32[2048]{0:T(1024)}, u32[]{:S(2)}) copy-start(f32[2048]{0:T(1024)} %copy-done.47) | copy-start | bytes 24580
  682.7 106.3 %copy-start.44 = (f32[2048]{0:T(1024)S(1)}, f32[2048]{0:T(1024)}, u32[]{:S(2)}) copy-start(f32[2048]{0:T(1024)} %copy-done.43) | copy-start | bytes 24580
  804.5 19.6 %copy-start.11 = (bf16[8192,128]{1,0:T(8,128)(2,1)S(1)}, bf16[8192,128]{1,0:T(8,128)(2,1)}, u32[]{:S(2)}) copy-start(bf16[8192,128]{1,0:T(8,128)(2,1)} %all-gather.2.cloned.1.call-done) | copy-start | bytes 6291460
  804.5 19.6 %copy-start.42 = (f32[8192]{0:T(1024)S(1)}, f32[8192]{0:T(1024)}, u32[]{:S(2)}) copy-start(f32[8192]{0:T(1024)} %get-tuple-element.1343) | copy-start | bytes 98308
  804.5 347.5 %reduce-scatter.2.cloned.1.call-start = ((), (), s32[]{:S(2)}) async-start(), calls=%async_computation.4 | async-start | bytes 4718592 | tf_op jit(solution)/shard_map/reduce_scatter | solution.py:291
  1060.6 101.3 %copy-start.27 = (f32[768,768]{1,0:T(8,128)S(1)}, f32[768,768]{1,0:T(8,128)}, u32[]{:S(2)}) copy-start(f32[768,768]{1,0:T(8,128)} %get-tuple-element.2138) | copy-start | bytes 7077892
  (55 other events, 260.4 us)
Sparse Core Ops, SparseCore 0:
  10.1 51.7 all-gather.1
  195.7 118.1 all-reduce.7
  356.2 119.7 all-reduce.9
  663.3 119.7 all-reduce.13
  804.6 256.0 all-reduce.11
  1064.7 87.2 reduce-scatter.1
where the time goes:
time: 1180 us; the launch traced here: 1170 us
  waiting for transfers between devices  638 us (54%)
  matrix products  279 us (24%)
  other arithmetic  115 us (10%)
  local copies, waits for them, and re-layouts  75.5 us (6%)
  blocking collectives  40.1 us (3%)
  between operations  17.5 us (1%)
    psum x1, waiting for transfers between devices, body(): lax.psum((grad_w_in, grad_b_in, grad_w_time, grad_gain1, grad_shift1, gra...  173 us
    psum x1, waiting for transfers between devices, body(): resid = hidden + lax.psum(attn_part, 'mp')  118 us
    psum x1, waiting for transfers between devices, body(): grad_act_two = lax.psum(grad_two_part, 'mp')  106 us
    psum x1, waiting for transfers between devices, body(): lax.psum(down_part.astype(jnp.bfloat16), 'mp').astype(jnp.float32)  100 us
    reduce_scatter x1, waiting for transfers between devices, body(): lax.psum_scatter(direct + norm_coeff * unit_rows, 'dp', scatter_dimension...  91.4 us
    dot_general x32, matrix products, probs_for(): jnp.einsum('qhd,khd->hqk', grad_blk, value_blk, preferred_element_type=jn...  59.4 us
    all_gather x1, waiting for transfers between devices, body(): whole_table = lax.all_gather(table, 'dp', axis=0, tiled=True)  48.5 us
    dot_general x16, matrix products, value_step(): jnp.einsum('hqk,khd->qhd', weights_bf, block_rows(values_all, k_index, bl...  45.2 us
  transfers between devices with their start and end apart: 6, of which 6 were waited for; matrix products, arithmetic and copies ran while one was open for 7% of the time, Pallas kernels for 0%

commit v1 on v0

--- a/solution.py
+++ b/solution.py
@@ -253,7 +253,7 @@
     grad_w_up = jnp.einsum("td,tf->df", act_two, grad_pre_r, preferred_element_type=jnp.float32)
     grad_b_up = jnp.sum(grad_pre_r.astype(jnp.float32), axis=0)
     grad_two_part = jnp.einsum("tf,df->td", grad_pre_r, w_up, preferred_element_type=jnp.float32)
-    grad_act_two = lax.psum(grad_two_part, "mp")
+    grad_act_two = jnp.sum(lax.all_gather(grad_two_part, "mp"), axis=0)
     grad_resid_norm, grad_gain2, grad_shift2 = norm_two_back(grad_act_two)
     grad_resid = cotangent + grad_resid_norm
     grad_attn_r = grad_resid.astype(jnp.bfloat16)

time: 1180 us -> 1240 us (1.051)
  other arithmetic: 115 us -> 140 us
  waiting for transfers between devices: 638 us -> 660 us
    all_gather x0 -> x1, waiting for transfers between devices: none -> 140 us  [body(): grad_act_two = jnp.sum(lax.all_gather(grad_two_part, 'mp'), axis=0)]
    psum x1 -> x0, waiting for transfers between devices: 106 us -> none  [body(): grad_act_two = lax.psum(grad_two_part, 'mp')]
    reduce_sum x0 -> x1, other arithmetic: none -> 12.6 us  [body(): grad_act_two = jnp.sum(lax.all_gather(grad_two_part, 'mp'), axis=0)]
    reduce_sum x3 -> x4, other arithmetic: 17.9 us -> 29.6 us  [layer_norm(): return centred * lax.rsqrt(variance + 1e-05) * gain_vec + shift_vec]
    unnamed x155 -> x153, local copies, waits for them, and re-layouts: 32.4 us -> 32.9 us
  transfers between devices with their start and end apart: 6 -> 6, of which waited for: 6 -> 6; matrix products, arithmetic and copies ran while one was open for 7% -> 8% of each run, Pallas kernels for 0% -> 0%
where the time goes in v1:
time: 1240 us; the launch traced here: 1220 us
  waiting for transfers between devices  660 us (53%)
  matrix products  280 us (23%)
  other arithmetic  140 us (11%)
  local copies, waits for them, and re-layouts  82.7 us (7%)
  blocking collectives  39.4 us (3%)
  between operations  17.6 us (1%)
    psum x1, waiting for transfers between devices, body(): lax.psum((grad_w_in, grad_b_in, grad_w_time, grad_gain1, grad_shift1, gra...  161 us
    all_gather x1, waiting for transfers between devices, body(): grad_act_two = jnp.sum(lax.all_gather(grad_two_part, 'mp'), axis=0)  140 us
    psum x1, waiting for transfers between devices, body(): resid = hidden + lax.psum(attn_part, 'mp')  118 us
    psum x1, waiting for transfers between devices, body(): lax.psum(down_part.astype(jnp.bfloat16), 'mp').astype(jnp.float32)  100 us
    reduce_scatter x1, waiting for transfers between devices, body(): lax.psum_scatter(direct + norm_coeff * unit_rows, 'dp', scatter_dimension...  91.4 us
    dot_general x32, matrix products, probs_for(): jnp.einsum('qhd,khd->hqk', grad_blk, value_blk, preferred_element_type=jn...  59.4 us
    all_gather x1, waiting for transfers between devices, body(): whole_table = lax.all_gather(table, 'dp', axis=0, tiled=True)  48.5 us
    dot_general x16, matrix products, value_step(): jnp.einsum('hqk,khd->qhd', weights_bf, block_rows(values_all, k_index, bl...  45.2 us
  transfers between devices with their start and end apart: 6, of which 6 were waited for; matrix products, arithmetic and copies ran while one was open for 8% of the time, Pallas kernels for 0%

profile of v1, /device:TPU:0, one launch (start us, length us, event | category | flops | bytes accessed | tf_op | source)
XLA Modules:
  0.0 1225.0 jit_solution(9801567382336779501)
XLA Ops:
  13.5 48.5 %all-gather.4.cloned.1.call-done = bf16[8192,128]{1,0:T(8,128)(2,1)} async-done(((bf16[1024,128]{1,0:T(8,128)(2,1)}), bf16[8192,128]{1,0:T(8,128)(2,1)}) %all-gather.4.cloned.1.call-update) | async-done | bytes 2097168 | tf_op jit(solution)/shard_map/all_gather | solution.py:209
  90.6 98.2 %while.123 = (s32[]{:T(128)}, bf16[4,512,3,64]{1,3,2,0:T(8,128)(2,1)}, f32[4,3,512]{2,1,0:T(4,128)}, f32[4,3,512]{2,1,0:T(4,128)}, s32[4]{0:T(128)S(1)}, /*index...) while((s32[]{:T(128)}, ...), condition=%wide.region_11.12_spmd, body=%wide.region_4.11_spmd.sunk | while | flops 312155648 | bytes 10699101 | solution.py:101
  100.9 12.5 %while.128 = (s32[]{:T(128)}, f32[512,3,64]{0,2,1:T(8,128)}, bf16[2048,3,64]{0,2,1:T(8,128)(2,1)S(1)}, s32[512]{0:T(512)S(1)}, s32[2048]{0:T(1024)S(1)}, /*index...) while((s32[]{:T(128)}, f32[512,3,64]{0,2,1:T(8,128)}, ...), condition=%wide.region_10.10_spmd.clone, body=%wide.region_9.9_spmd.clone.sunk | while | flops 205717504 | bytes 1926848 | solution.py:96
  125.4 12.5 %while.128 = (s32[]{:T(128)}, f32[512,3,64]{0,2,1:T(8,128)}, bf16[2048,3,64]{0,2,1:T(8,128)(2,1)S(1)}, s32[512]{0:T(512)S(1)}, s32[2048]{0:T(1024)S(1)}, /*index...) while((s32[]{:T(128)}, f32[512,3,64]{0,2,1:T(8,128)}, ...), condition=%wide.region_10.10_spmd.clone, body=%wide.region_9.9_spmd.clone.sunk | while | flops 205717504 | bytes 1926848 | solution.py:96
  149.9 12.5 %while.128 = (s32[]{:T(128)}, f32[512,3,64]{0,2,1:T(8,128)}, bf16[2048,3,64]{0,2,1:T(8,128)(2,1)S(1)}, s32[512]{0:T(512)S(1)}, s32[2048]{0:T(1024)S(1)}, /*index...) while((s32[]{:T(128)}, f32[512,3,64]{0,2,1:T(8,128)}, ...), condition=%wide.region_10.10_spmd.clone, body=%wide.region_9.9_spmd.clone.sunk | while | flops 205717504 | bytes 1926848 | solution.py:96
  174.4 12.5 %while.128 = (s32[]{:T(128)}, f32[512,3,64]{0,2,1:T(8,128)}, bf16[2048,3,64]{0,2,1:T(8,128)(2,1)S(1)}, s32[512]{0:T(512)S(1)}, s32[2048]{0:T(1024)S(1)}, /*index...) while((s32[]{:T(128)}, f32[512,3,64]{0,2,1:T(8,128)}, ...), condition=%wide.region_10.10_spmd.clone, body=%wide.region_9.9_spmd.clone.sunk | while | flops 205717504 | bytes 1926848 | solution.py:96
  195.7 118.2 %all-reduce.7.cloned.1.call-done = f32[2048,768]{0,1:T(8,128)} async-done(((f32[2048,768]{0,1:T(8,128)}), f32[2048,768]{0,1:T(8,128)}) %all-reduce.7.cloned.1.call-update) | async-done | bytes 6291472 | tf_op jit(solution)/shard_map/psum | solution.py:237
  323.0 18.8 %multiply_convert_fusion = (bf16[2048,768]{1,0:T(8,128)(2,1)}, f32[2048,768]{1,0:T(8,128)}, f32[2048,768]{1,0:T(8,128)}) fusion(f32[768]{0:T(1024)S(1)} %copy-done.62, bf16[2048,768]{0,1:T(8,128)(2,1)S(1)} %add_convert_fusion.2, bf16[768,768]{1,0:T(8,128)(2,1)S(1)} %copy-done), kind=kOutput, calls=%fused_computation.93 | convolution fusion | flops 2519728128 | bytes 20057088 | tf_op jit(solution)/shard_map/dot_general | solution.py:240
  371.1 140.2 %all-gather.6.cloned.1.call-done = f32[8192,768]{1,0:T(8,128)} async-done(((f32[2048,768]{1,0:T(8,128)}), f32[8192,768]{1,0:T(8,128)}) %all-gather.6.cloned.1.call-update) | async-done | bytes 25165840 | tf_op jit(solution)/shard_map/all_gather | solution.py:256
  511.3 12.6 %reduce_sum.235 = f32[2048,768]{1,0:T(8,128)} reduce(f32[4,2048,768]{2,1,0:T(8,128)} %bitcast.205, f32[]{:T(128)} %constant.325.clone.1), dimensions={0}, to_apply=%region_16.17 | reduce | flops 4718592 | bytes 31457284 | tf_op jit(solution)/shard_map/reduce_sum | solution.py:256
  547.4 161.6 %while.126 = (s32[]{:T(128)}, bf16[2048,3,64]{0,2,1:T(8,128)(2,1)}, f32[2048,3,64]{0,2,1:T(8,128)}, f32[2048,3,64]{0,2,1:T(8,128)S(1)}, bf16[2048,3,64]{0,2,1:T(...) while((s32[]{:T(128)}, bf16[2048,3,64]{0,2,1:T(8,128)(2,1)}, ...), condition=%wide.region_25.26_spmd, body=%wide.region_19.25_spmd.sunk | while | flops 716768768 | bytes 27696096 | solution.py:185
  549.4 12.6 %while.129 = (s32[]{:T(128)}, f32[3,512]{1,0:T(4,128)S(1)}, bf16[2048,3,64]{0,2,1:T(8,128)(2,1)}, bf16[512,3,64]{0,2,1:T(8,128)(2,1)S(1)}, s32[512]{0:T(512)S(1)...) while((s32[]{:T(128)}, f32[3,512]{1,0:T(4,128)S(1)}, ...), condition=%wide.region_22.22_spmd.clone, body=%wide.region_20.21_spmd.clone.sunk | while | flops 206308864 | bytes 7647441 | solution.py:134
  562.0 25.2 %while.130 = (s32[]{:T(128)}, f32[512,3,64]{0,2,1:T(8,128)S(1)}, f32[2048,3,64]{0,2,1:T(8,128)}, f32[2048,3,64]{0,2,1:T(8,128)S(1)}, bf16[2048,3,64]{0,2,1:T(8,1...) while((s32[]{:T(128)}, f32[512,3,64]{0,2,1:T(8,128)S(1)}, ...), condition=%wide.region_24.24_spmd.clone, body=%wide.region_23.23_spmd.clone.sunk | while | flops 510459904 | bytes 18446580 | solution.py:180
  589.7 12.6 %while.129 = (s32[]{:T(128)}, f32[3,512]{1,0:T(4,128)S(1)}, bf16[2048,3,64]{0,2,1:T(8,128)(2,1)}, bf16[512,3,64]{0,2,1:T(8,128)(2,1)S(1)}, s32[512]{0:T(512)S(1)...) while((s32[]{:T(128)}, f32[3,512]{1,0:T(4,128)S(1)}, ...), condition=%wide.region_22.22_spmd.clone, body=%wide.region_20.21_spmd.clone.sunk | while | flops 206308864 | bytes 7647441 | solution.py:134
  602.3 25.2 %while.130 = (s32[]{:T(128)}, f32[512,3,64]{0,2,1:T(8,128)S(1)}, f32[2048,3,64]{0,2,1:T(8,128)}, f32[2048,3,64]{0,2,1:T(8,128)S(1)}, bf16[2048,3,64]{0,2,1:T(8,1...) while((s32[]{:T(128)}, f32[512,3,64]{0,2,1:T(8,128)S(1)}, ...), condition=%wide.region_24.24_spmd.clone, body=%wide.region_23.23_spmd.clone.sunk | while | flops 510459904 | bytes 18446580 | solution.py:180
  630.1 12.6 %while.129 = (s32[]{:T(128)}, f32[3,512]{1,0:T(4,128)S(1)}, bf16[2048,3,64]{0,2,1:T(8,128)(2,1)}, bf16[512,3,64]{0,2,1:T(8,128)(2,1)S(1)}, s32[512]{0:T(512)S(1)...) while((s32[]{:T(128)}, f32[3,512]{1,0:T(4,128)S(1)}, ...), condition=%wide.region_22.22_spmd.clone, body=%wide.region_20.21_spmd.clone.sunk | while | flops 206308864 | bytes 7647441 | solution.py:134
  642.7 25.2 %while.130 = (s32[]{:T(128)}, f32[512,3,64]{0,2,1:T(8,128)S(1)}, f32[2048,3,64]{0,2,1:T(8,128)}, f32[2048,3,64]{0,2,1:T(8,128)S(1)}, bf16[2048,3,64]{0,2,1:T(8,1...) while((s32[]{:T(128)}, f32[512,3,64]{0,2,1:T(8,128)S(1)}, ...), condition=%wide.region_24.24_spmd.clone, body=%wide.region_23.23_spmd.clone.sunk | while | flops 510459904 | bytes 18446580 | solution.py:180
  670.5 12.6 %while.129 = (s32[]{:T(128)}, f32[3,512]{1,0:T(4,128)S(1)}, bf16[2048,3,64]{0,2,1:T(8,128)(2,1)}, bf16[512,3,64]{0,2,1:T(8,128)(2,1)S(1)}, s32[512]{0:T(512)S(1)...) while((s32[]{:T(128)}, f32[3,512]{1,0:T(4,128)S(1)}, ...), condition=%wide.region_22.22_spmd.clone, body=%wide.region_20.21_spmd.clone.sunk | while | flops 206308864 | bytes 7647441 | solution.py:134
  683.0 25.2 %while.130 = (s32[]{:T(128)}, f32[512,3,64]{0,2,1:T(8,128)S(1)}, f32[2048,3,64]{0,2,1:T(8,128)}, f32[2048,3,64]{0,2,1:T(8,128)S(1)}, bf16[2048,3,64]{0,2,1:T(8,1...) while((s32[]{:T(128)}, f32[512,3,64]{0,2,1:T(8,128)S(1)}, ...), condition=%wide.region_24.24_spmd.clone, body=%wide.region_23.23_spmd.clone.sunk | while | flops 510459904 | bytes 18446580 | solution.py:180
  737.3 100.1 %all-reduce.11.cloned.1.call-done = (bf16[2048,768]{0,1:T(8,128)(2,1)}, bf16[2048,768]{0,1:T(8,128)(2,1)}) async-done(((bf16[2048,768]{0,1:T(8,128)(2,1)}, bf16[2048,768]{0,1:T(8,128)(2,1)}), (bf16[2048,768]{0,1:T(8,128)(2,1)}, bf16[2048,768]{0,1:T(8,128)(2,1)})) %all-reduce.11.cloned.1.call-update) | async-done | bytes 6291472 | tf_op jit(solution)/shard_map/psum | solution.py:244
  865.3 13.1 %scatter_custom_fusion = f32[8193,128]{1,0:T(8,128)} fusion(s32[2048]{0:T(1024)} %get-tuple-element.1361, f32[]{:T(128)} %constant.325.clone.1, f32[2048,128]{1,0:T(8,128)} %get-tuple-element.1369, f32[]{:T(128)S(6)} %div.136), kind=kCustom, calls=%fused_computation.122 | custom fusion | flops 524288 | bytes 5243908 | tf_op jit(solution)/shard_map/scatter-add | solution.py:290
  914.8 39.4 %all-reduce = (f32[768]{0:T(1024)}, f32[768]{0:T(1024)}, f32[768]{0:T(1024)}, f32[768]{0:T(1024)}, f32[768]{0:T(1024)}, /*index=5*/f32[768]{0:T(1024)}, f32[768]{0:T(1024)}) all-reduce(f32[768]{0:T(1024)S(1)} %get-tuple-element.1338, f32[768]{0:T(1024)S(1)} %get-tuple-element.1201, ...), channel_id=1, replica_groups=mesh['dp'=8,'mp'=4] {'dp'}, use_global_device_ids=true, to_apply=%region_34.35 | all-reduce | flops 5376 | bytes 43008 | tf_op jit(solution)/shard_map/psum | solution.py:295
  954.2 160.7 %all-reduce.9.cloned.1.call-done = (f32[128,768]{1,0:T(8,128)}, f32[128,768]{1,0:T(8,128)}, f32[3,768,192]{1,2,0:T(8,128)}, f32[192,768]{1,0:T(8,128)}, f32[768,768]{1,0:T(8,128)}, /*index=5*/f32[768,768]{1,0:T(8,128)}) async-done(((f32[128,768]{1,0:T(8,128)}, f32[128,768]{1,0:T(8,128)}, f32[3,768,192]{1,2,0:T(8,128)}, f32[192,768]{1,0:T(8,128)}, f32[768,768]{1,0:T(8,128)}, ...) | async-done | bytes 7864336 | tf_op jit(solution)/shard_map/psum | solution.py:295
  1115.0 91.4 %reduce-scatter.2.cloned.1.call-done = f32[1024,128]{1,0:T(8,128)} async-done(((f32[8192,128]{1,0:T(8,128)}), f32[1024,128]{1,0:T(8,128)}) %reduce-scatter.2.cloned.1.call-update) | async-done | bytes 524304 | tf_op jit(solution)/shard_map/reduce_scatter | solution.py:291
  (644 shorter events, 488.6 us)
Async XLA Ops:
  7.2 315.8 %copy-start = (bf16[768,768]{1,0:T(8,128)(2,1)S(1)}, bf16[768,768]{1,0:T(8,128)(2,1)}, u32[]{:S(2)}) copy-start(bf16[768,768]{1,0:T(8,128)(2,1)} %param.45) | copy-start | bytes 3538948
  7.2 54.8 %all-gather.4.cloned.1.call-start = ((), (), s32[]{:S(2)}) async-start(), calls=%async_computation.1 | async-start | bytes 2359296 | tf_op jit(solution)/shard_map/all_gather | solution.py:209
  7.9 305.9 %all-reduce.7.cloned.1.call-start = ((), (), s32[]{:S(2)}) async-start(), calls=%async_computation.2 | async-start | bytes 12582912 | tf_op jit(solution)/shard_map/psum | solution.py:237
  9.4 68.8 %copy-start.51 = (pred[2048]{0:T(1024)(128)(4,1)}, pred[2048]{0:T(1024)(128)(4,1)S(1)}, u32[]{:S(2)}) copy-start(pred[2048]{0:T(1024)(128)(4,1)S(1)} %compare_and_fusion) | copy-start | bytes 6148
  11.4 66.8 %copy-start.39 = (f32[2048]{0:T(1024)}, f32[2048]{0:T(1024)S(1)}, u32[]{:S(2)}) copy-start(f32[2048]{0:T(1024)S(1)} %get-tuple-element.1363) | copy-start | bytes 24580
  13.5 69.2 %copy-start.23 = (bf16[2048,64]{0,1:T(8,128)(2,1)}, bf16[2048,64]{0,1:T(8,128)(2,1)S(1)}, u32[]{:S(2)}) copy-start(bf16[2048,64]{0,1:T(8,128)(2,1)S(1)} %get-tuple-element.1359) | copy-start | bytes 786436
  13.5 69.2 %copy-start.25 = (bf16[2048,64]{0,1:T(8,128)(2,1)}, bf16[2048,64]{0,1:T(8,128)(2,1)S(1)}, u32[]{:S(2)}) copy-start(bf16[2048,64]{0,1:T(8,128)(2,1)S(1)} %get-tuple-element.1360) | copy-start | bytes 786436
  90.6 101.3 %copy-start.29 = (bf16[192,768]{1,0:T(8,128)(2,1)S(1)}, bf16[192,768]{1,0:T(8,128)(2,1)}, u32[]{:S(2)}) copy-start(bf16[192,768]{1,0:T(8,128)(2,1)} %param.42) | copy-start | bytes 884740
  195.6 315.7 %all-gather.6.cloned.1.call-start = ((), (), s32[]{:S(2)}) async-start(), calls=%async_computation.4 | async-start | bytes 31457280 | tf_op jit(solution)/shard_map/all_gather | solution.py:256
  320.9 20.9 %slice-start.2 = ((s8[6291456]{0:T(1024)(128)(4,1)}), s8[4194304]{0:T(1024)(128)(4,1)S(1)}, s32[]{:S(2)}) async-start(s8[6291456]{0:T(1024)(128)(4,1)} %bitcast.206), calls=%async_computation.9 | async-start | bytes 8388608
  322.9 18.8 %copy-start.21 = (bf16[2048,768]{0,1:T(8,128)(2,1)}, bf16[2048,768]{0,1:T(8,128)(2,1)S(1)}, u32[]{:S(2)}) copy-start(bf16[2048,768]{0,1:T(8,128)(2,1)S(1)} %add_convert_fusion.2) | copy-start | bytes 9437188
  323.0 18.8 %slice-start.3 = ((s8[6291456]{0:T(1024)(128)(4,1)}), s8[2097152]{0:T(1024)(128)(4,1)S(1)}, s32[]{:S(2)}) async-start(s8[6291456]{0:T(1024)(128)(4,1)} %bitcast.206), calls=%async_computation.10 | async-start | bytes 4194304
  323.0 18.8 %copy-start.60 = (bf16[768,768]{1,0:T(8,128)(2,1)S(1)}, bf16[768,768]{1,0:T(8,128)(2,1)}, u32[]{:S(2)}) copy-start(bf16[768,768]{1,0:T(8,128)(2,1)} %param.47) | copy-start | bytes 3538948
  356.1 481.2 %all-reduce.11.cloned.1.call-start = ((), (), s32[]{:S(2)}) async-start(), calls=%async_computation.6 | async-start | bytes 12582912 | tf_op jit(solution)/shard_map/psum | solution.py:244
  717.6 397.4 %all-reduce.9.cloned.1.call-start = ((), (), s32[]{:S(2)}) async-start(), calls=%async_computation.5 | async-start | bytes 15728640 | tf_op jit(solution)/shard_map/psum | solution.py:295
  734.0 103.4 %copy-start.38 = (f32[2048]{0:T(1024)S(1)}, f32[2048]{0:T(1024)}, u32[]{:S(2)}) copy-start(f32[2048]{0:T(1024)} %copy-done.37) | copy-start | bytes 24580
  734.0 103.4 %copy-start.50 = (f32[768]{0:T(1024)S(1)}, f32[768]{0:T(1024)}, u32[]{:S(2)}) copy-start(f32[768]{0:T(1024)} %param.39) | copy-start | bytes 9220
  734.0 114.9 %slice-start.6 = ((s8[6291456]{0:T(1024)(128)(4,1)}), s8[2097152]{0:T(1024)(128)(4,1)S(1)}, s32[]{:S(2)}) async-start(s8[6291456]{0:T(1024)(128)(4,1)} %bitcast.210), calls=%async_computation.13 | async-start | bytes 4194304
  737.3 105.9 %copy-start.48 = (f32[2048]{0:T(1024)S(1)}, f32[2048]{0:T(1024)}, u32[]{:S(2)}) copy-start(f32[2048]{0:T(1024)} %copy-done.47) | copy-start | bytes 24580
  737.3 105.9 %copy-start.44 = (f32[2048]{0:T(1024)S(1)}, f32[2048]{0:T(1024)}, u32[]{:S(2)}) copy-start(f32[2048]{0:T(1024)} %copy-done.43) | copy-start | bytes 24580
  858.8 19.6 %copy-start.11 = (bf16[8192,128]{1,0:T(8,128)(2,1)S(1)}, bf16[8192,128]{1,0:T(8,128)(2,1)}, u32[]{:S(2)}) copy-start(bf16[8192,128]{1,0:T(8,128)(2,1)} %all-gather.4.cloned.1.call-done) | copy-start | bytes 6291460
  858.8 19.6 %copy-start.42 = (f32[8192]{0:T(1024)S(1)}, f32[8192]{0:T(1024)}, u32[]{:S(2)}) copy-start(f32[8192]{0:T(1024)} %get-tuple-element.1357) | copy-start | bytes 98308
  858.8 347.6 %reduce-scatter.2.cloned.1.call-start = ((), (), s32[]{:S(2)}) async-start(), calls=%async_computation.3 | async-start | bytes 4718592 | tf_op jit(solution)/shard_map/reduce_scatter | solution.py:291
  1114.9 101.3 %copy-start.27 = (f32[768,768]{1,0:T(8,128)S(1)}, f32[768,768]{1,0:T(8,128)}, u32[]{:S(2)}) copy-start(f32[768,768]{1,0:T(8,128)} %get-tuple-element.2152) | copy-start | bytes 7077892
  (54 other events, 263.0 us)
Sparse Core Ops, SparseCore 0:
  10.1 51.7 all-gather.3
  195.7 118.1 all-reduce.6
  356.2 154.9 all-gather.5
  717.7 119.6 all-reduce.10
  858.9 256.0 all-reduce.8
  1119.0 87.2 reduce-scatter.1
